TPU v7x, 32 devices: a whole 2x2x4 slice. The times are simulated.
32 devices in a mesh: parts: 2 (over x), dp: 4 (over y, core), shard: 4 (over z).
Axes of the slice: x: 2, y: 2, z: 4, core: 2. Of those that a mesh axis runs over, the one named last changes fastest.
Arguments:
- projected: bfloat16 [7680, 7680], P(('parts', 'dp', 'shard')), parts along dimension 0, may hold values from -4 to 4
- residual: bfloat16 [7680, 2560], P(('parts', 'dp', 'shard')), parts along dimension 0, may hold values from -6 to 6
- out_weight: bfloat16 [2560, 2560], P(None, 'shard'), may hold values from -0.125 to 0.125
- probe_weight: bfloat16 [2, 2560, 8], replicated, may hold values from -0.125 to 0.125
- labels: int32 [7680], P(('parts', 'dp', 'shard')), parts along dimension 0, may hold values from 0 to 7
- lengths: int32 [32, 9], P(('parts', 'dp', 'shard')), parts along dimension 0, may hold values from 12 to 48, as said below
- destination: int32 [32, 9], P(('parts', 'dp', 'shard')), parts along dimension 0, may hold values from 0 to 3, as said below
Outputs:
- hidden_rows: bfloat16 [18432, 2560], P(('parts', 'dp', 'shard')), parts along dimension 0
- probe_grad: float32 [4, 2560, 8], P('parts'), parts along dimension 0
There are 2 independent parts, one for each index of `parts`. A program takes and returns all parts, laid end to end along the dimension named above; an argument that names none is the same for every part. Nothing has to cross between parts.
Inputs may be any that keep to these rules, and one draw needn't show every extreme that they name: Each row of lengths sums to 240 and holds exactly one protein of length 48. `destination`: A loader assigns at most 3 proteins to any one dp index; in every shard column one dp index is assigned exactly 3 proteins by every loader of that column.
All inputs are finite; a program needn't handle non-finite values.
Results may differ from a plain program's by a relative error of at most 0.0031.
Values may be sent and summed in bfloat16 or wider, within the bound.
No kernel may reach another device: no remote copies, remote signals or barrier semaphores. Data moves between devices by JAX's collectives and lax.ppermute only.
A program may use at most 128 MiB of HBM per device.

v0:
```python
import jax
import jax.numpy as jnp
from jax import lax
from jax.sharding import PartitionSpec as P

HS = 128
CLASSES = 8
LMAX = 48
TOK_DEV = 240


def attend(blocks, block_lengths):
    block_count = blocks.shape[0]
    span_rows = blocks.shape[1]
    head_width = blocks.shape[2] // 3
    head_count = head_width // HS
    queries = blocks[:, :, :head_width].reshape(block_count, span_rows, head_count, HS)
    key_rows = blocks[:, :, head_width : 2 * head_width].reshape(
        block_count, span_rows, head_count, HS
    )
    value_rows = blocks[:, :, 2 * head_width :].reshape(block_count, span_rows, head_count, HS)
    scores = jnp.einsum(
        "plhs,pmhs->phlm", queries, key_rows, preferred_element_type=jnp.float32
    ) * HS ** (-0.5)
    keep_mask = (jnp.arange(span_rows, dtype=jnp.int32)[None, :] < block_lengths[:, None]).astype(
        jnp.float32
    )
    weights = jnp.exp(scores) * keep_mask[:, None, None, :]
    denominator = (
        jnp.sum(weights, axis=-1, keepdims=True)
        + (block_lengths == 0).astype(jnp.float32)[:, None, None, None]
    )
    weight_low = (weights / denominator).astype(jnp.bfloat16)
    attended = jnp.einsum(
        "phlm,pmhs->plhs", weight_low, value_rows, preferred_element_type=jnp.float32
    )
    return attended.reshape(block_count * span_rows, head_width).astype(jnp.bfloat16)


def project(attended, out_weight):
    return jnp.dot(
        attended,
        lax.all_gather(out_weight, "shard", axis=1, tiled=True),
        preferred_element_type=jnp.float32,
    )


def probe_terms(represent_x, represent_h, label_rows, keep_mask, probe_weight):
    one_hot = (label_rows[:, None] == jnp.arange(CLASSES, dtype=jnp.int32)[None, :]).astype(
        jnp.float32
    )
    collected = []
    for which, represent in enumerate((represent_x, represent_h)):
        logits = jnp.dot(represent, probe_weight[which], preferred_element_type=jnp.float32)
        exponent = jnp.exp(logits)
        likelihood = exponent / jnp.sum(exponent, axis=1, keepdims=True)
        mismatch = ((likelihood - one_hot) * keep_mask[:, None] / TOK_DEV).astype(jnp.bfloat16)
        collected.append(
            lax.dot_general(
                represent, mismatch, (((0,), (0,)), ((), ())), preferred_element_type=jnp.float32
            )
        )
    return jnp.stack(collected)


def per_device(projected, residual, out_weight, probe_weight, labels, lengths, destination):
    group_size = lax.axis_size("dp")
    prot_count = lengths.shape[1]
    slot_count = -(-prot_count // group_size)
    tok_count = projected.shape[0]
    lens_own = lengths[0]
    dest_own = destination[0]
    starts = jnp.cumsum(lens_own) - lens_own
    offsets = jnp.arange(LMAX, dtype=jnp.int32)
    positions = jnp.arange(prot_count, dtype=jnp.int32)
    same_dest = dest_own[:, None] == dest_own[None, :]
    earlier = positions[:, None] > positions[None, :]
    slot_rank = jnp.sum((same_dest & earlier).astype(jnp.int32), axis=1)
    slot_match = (
        dest_own[None, None, :] == jnp.arange(group_size, dtype=jnp.int32)[:, None, None]
    ) & (slot_rank[None, None, :] == jnp.arange(slot_count, dtype=jnp.int32)[None, :, None])
    match_int = slot_match.astype(jnp.int32)
    slot_start = jnp.sum(match_int * starts, axis=2)
    slot_len = jnp.sum(match_int * lens_own, axis=2)
    block_count = group_size * slot_count
    row_index = jnp.minimum(slot_start[:, :, None] + offsets, tok_count - 1).reshape(
        group_size, slot_count * LMAX
    )
    live_rows = (offsets[None, None, :] < slot_len[:, :, None]).reshape(
        group_size, slot_count * LMAX
    )
    rows_send = jnp.where(live_rows[:, :, None], jnp.take(projected, row_index, axis=0), 0)
    resid_send = jnp.where(live_rows[:, :, None], jnp.take(residual, row_index, axis=0), 0)
    label_send = jnp.where(live_rows, jnp.take(labels, row_index), 0)
    got_labels, got_lengths = (
        lax.all_to_all(label_send, "dp", split_axis=0, concat_axis=0, tiled=True),
        lax.all_to_all(slot_len, "dp", split_axis=0, concat_axis=0, tiled=True),
    )
    got_rows, got_resid = (
        lax.all_to_all(rows_send, "dp", split_axis=0, concat_axis=0, tiled=True),
        lax.all_to_all(resid_send, "dp", split_axis=0, concat_axis=0, tiled=True),
    )
    lengths_recv = got_lengths.reshape(block_count)
    attended = attend(got_rows.reshape(block_count, LMAX, -1), lengths_recv)
    keep_mask = (offsets[None, :] < lengths_recv[:, None]).astype(jnp.float32).reshape(-1)
    represent = got_resid.reshape(block_count * LMAX, -1)
    mixed_rows = project(attended, out_weight) + represent.astype(jnp.float32)
    hidden = (mixed_rows * keep_mask[:, None]).astype(jnp.bfloat16)
    grad_terms = probe_terms(represent, hidden, got_labels.reshape(-1), keep_mask, probe_weight)
    grad_sum = lax.psum(grad_terms, ("dp", "shard"))
    return (hidden, grad_sum)


def solution(mesh):
    return jax.shard_map(
        per_device,
        mesh=mesh,
        in_specs=(
            P(("parts", "dp", "shard"), None),
            P(("parts", "dp", "shard"), None),
            P(None, "shard"),
            P(),
            P(("parts", "dp", "shard")),
            P(("parts", "dp", "shard"), None),
            P(("parts", "dp", "shard"), None),
        ),
        out_specs=(P(("parts", "dp", "shard"), None), P("parts", None, None)),
        check_vma=False,
    )
```

profile of v0, /device:TPU:8, one launch (start us, length us, event | category | flops | bytes accessed | tf_op | source)
XLA Modules:
  0.0 349.7 jit_solution(5877579920904036037)
XLA Ops:
  7.2 0.7 all-gather.2.cloned.1.call-update
  8.3 0.2 fusion.37
  8.5 0.7 copy.27
  9.2 3.2 all-to-all-start.1
  13.4 4.2 %gather_fusion.1 = bf16[576,2560]{1,0:T(8,128)(2,1)} fusion(bf16[240,2560]{1,0:T(8,128)(2,1)S(1)} %copy-done, s32[1024]{0:T(1024)S(1)} %pad_clamp_fusion), kind=kCustom, calls=%fused_computation.1 | custom fusion | bytes 5900544 | tf_op jit(solution)/shard_map/jit(_take)/gather | solution.py:93
  17.6 3.9 %gather_fusion.2 = s32[576]{0:T(1024)S(1)} fusion(s32[240]{0:T(256)S(1)} %copy-done.2, s32[1024]{0:T(1024)S(1)} %pad_clamp_fusion), kind=kCustom, calls=%fused_computation.2 | custom fusion | bytes 6912 | tf_op jit(solution)/shard_map/jit(_take)/gather | solution.py:94
  21.6 0.6 copy.31
  22.3 3.3 all-to-all-start.3
  25.5 4.2 %select_select_fusion.1 = bf16[4,144,2560]{2,1,0:T(8,128)(2,1)} fusion(bf16[4,144,2560]{2,1,0:T(8,128)(2,1)} %bitcast.61, pred[4,144]{1,0:T(4,128)(4,1)S(1)} %get-tuple-element.8, pred[4,144]{1,0:T(4,128)(4,1)S(1)} %get-tuple-element.7), kind=kLoop, calls=%fused_computation.23 | loop fusion | flops 2949120 | bytes 5899392 | tf_op jit(solution)/shard_map/jit(_where)/select_n | solution.py:93
  29.7 22.4 %gather_fusion = bf16[576,7680]{1,0:T(8,128)(2,1)} fusion(bf16[240,7680]{1,0:T(8,128)(2,1)} %param.7, s32[1024]{0:T(1024)S(1)} %pad_clamp_fusion), kind=kCustom, calls=%fused_computation | custom fusion | bytes 17697024 | tf_op jit(solution)/shard_map/jit(_take)/gather | solution.py:92
  52.1 4.6 %all-to-all-start.2 = ((bf16[4,144,2560]{2,1,0:T(8,128)(2,1)}), bf16[4,144,2560]{2,1,0:T(8,128)(2,1)}, u32[]{:S(2)}, u32[]{:S(2)}) async-start(bf16[4,144,2560]{2,1,0:T(8,128)(2,1)} %select_select_fusion.1), calls=%async_computation.2 | async-start | bytes 5898240 | tf_op jit(solution)/shard_map/all_to_all | solution.py:101
  56.8 8.1 %select_select_fusion = bf16[4,144,7680]{2,1,0:T(8,128)(2,1)} fusion(bf16[4,144,7680]{2,1,0:T(8,128)(2,1)} %bitcast.60, pred[4,144]{1,0:T(4,128)(4,1)S(1)} %get-tuple-element.8, pred[4,144]{1,0:T(4,128)(4,1)S(1)} %get-tuple-element.7), kind=kLoop, calls=%fused_computation.3 | loop fusion | flops 8847360 | bytes 17695872 | tf_op jit(solution)/shard_map/jit(_where)/select_n | solution.py:92
  64.9 26.7 %all-to-all-done.2 = bf16[4,144,2560]{2,1,0:T(8,128)(2,1)} async-done(((bf16[4,144,2560]{2,1,0:T(8,128)(2,1)}), bf16[4,144,2560]{2,1,0:T(8,128)(2,1)}, u32[]{:S(2)}, u32[]{:S(2)}) %all-to-all-start.2) | async-done | bytes 2949152 | tf_op jit(solution)/shard_map/all_to_all | solution.py:101
  91.6 5.7 %all-to-all-start = ((bf16[4,144,7680]{2,1,0:T(8,128)(2,1)}), bf16[4,144,7680]{2,1,0:T(8,128)(2,1)}, u32[]{:S(2)}, u32[]{:S(2)}) async-start(bf16[4,144,7680]{2,1,0:T(8,128)(2,1)} %select_select_fusion), calls=%async_computation | async-start | bytes 17694720 | tf_op jit(solution)/shard_map/all_to_all | solution.py:100
  97.3 0.2 all-reduce.2.cloned.1.call-start
  97.6 0.5 broadcast.237
  98.1 0.7 reduce.4
  99.1 2.7 fusion.43
  101.8 2.3 convolution_bitcast_fusion.1
  104.1 91.3 %all-to-all-done = bf16[4,144,7680]{2,1,0:T(8,128)(2,1)} async-done(((bf16[4,144,7680]{2,1,0:T(8,128)(2,1)}), bf16[4,144,7680]{2,1,0:T(8,128)(2,1)}, u32[]{:S(2)}, u32[]{:S(2)}) %all-to-all-start) | async-done | bytes 8847392 | tf_op jit(solution)/shard_map/all_to_all | solution.py:100
  195.4 4.0 %slice_bitcast_fusion.2 = (bf16[12,6,20,8,128]{4,3,2,1,0:T(8,128)(2,1)S(1)}, bf16[12,6,20,8,128]{4,3,2,1,0:T(8,128)(2,1)S(1)}, bf16[12,6,20,8,128]{4,3,2,1,0:T(8,128)(2,1)S(1)}) fusion(bf16[12,48,7680]{2,1,0:T(8,128)(2,1)} %bitcast.5), kind=kLoop, calls=%fused_computation.22 | loop fusion | bytes 17694720
  199.4 1.7 fusion
  201.2 2.0 convert_bitcast_fusion
  203.2 2.6 copy.30
  205.8 28.8 %all-gather.2.cloned.1.call-done = bf16[2560,2560]{1,0:T(8,128)(2,1)} async-done(((bf16[2560,640]{1,0:T(8,128)(2,1)}), bf16[2560,2560]{1,0:T(8,128)(2,1)}) %all-gather.2.cloned.1.call-update) | async-done | bytes 13107216 | tf_op jit(solution)/shard_map/all_gather | solution.py:43
  234.6 12.4 %multiply_convert_fusion = bf16[576,2560]{1,0:T(8,128)(2,1)S(1)} fusion(bf16[576,2560]{1,0:T(8,128)(2,1)} %bitcast.9, bf16[2560,2560]{1,0:T(8,128)(2,1)} %all-gather.2.cloned.1.call-done, bf16[72,8,20,128]{3,2,1,0:T(8,128)(2,1)} %bitcast.62, f32[576]{0:T(1024)S(1)} %reshape.360), kind=kOutput, calls=%fused_computation.4 | convolution fusion | flops 7555645440 | bytes 21956864 | tf_op jit(solution)/shard_map/dot_general | solution.py:41
  246.9 0.9 fusion.42
  247.8 0.5 convolution_bitcast_fusion
  248.3 0.2 copy-done.3
  248.5 0.7 pad_maximum_fusion
  249.2 92.0 %all-reduce.2.cloned.1.call-done = f32[2,2560,8]{1,2,0:T(8,128)} async-done(((f32[2,2560,8]{1,2,0:T(8,128)}), f32[2,2560,8]{1,2,0:T(8,128)}) %all-reduce.2.cloned.1.call-update) | async-done | bytes 163856 | tf_op jit(solution)/shard_map/psum | solution.py:110
  341.3 1.6 copy.62
  (46 shorter events, 1.9 us)
Async XLA Ops:
  7.2 6.2 %copy-start = (bf16[240,2560]{1,0:T(8,128)(2,1)S(1)}, bf16[240,2560]{1,0:T(8,128)(2,1)}, u32[]{:S(2)}) copy-start(bf16[240,2560]{1,0:T(8,128)(2,1)} %param.8) | copy-start | bytes 3686404
  7.2 0.8 copy-start.5
  7.2 0.9 copy-start.6
  7.2 227.4 %all-gather.2.cloned.1.call-start = ((), (), s32[]{:S(2)}) async-start(), calls=%async_computation.4 | async-start | bytes 16384000 | tf_op jit(solution)/shard_map/all_gather | solution.py:43
  9.2 13.1 %all-to-all-start.1 = ((s32[4,1,3]{2,1,0:T(1,128)}), s32[4,1,3]{2,1,0:T(1,128)S(1)}, u32[]{:S(2)}, u32[]{:S(2)}) async-start(s32[4,1,3]{2,1,0:T(1,128)} %copy.27), calls=%async_computation.1 | async-start | bytes 4096 | tf_op jit(solution)/shard_map/all_to_all | solution.py:97
  13.4 4.2 %copy-start.2 = (s32[240]{0:T(256)S(1)}, s32[240]{0:T(256)}, u32[]{:S(2)}) copy-start(s32[240]{0:T(256)} %param.11) | copy-start | bytes 2884
  22.3 29.9 %all-to-all-start.3 = ((s32[4,1,144]{2,1,0:T(1,128)}), s32[4,1,144]{2,1,0:T(1,128)S(1)}, u32[]{:S(2)}, u32[]{:S(2)}) async-start(s32[4,1,144]{2,1,0:T(1,128)} %copy.31), calls=%async_computation.3 | async-start | bytes 8192 | tf_op jit(solution)/shard_map/all_to_all | solution.py:96
  52.1 39.5 %all-to-all-start.2 = ((bf16[4,144,2560]{2,1,0:T(8,128)(2,1)}), bf16[4,144,2560]{2,1,0:T(8,128)(2,1)}, u32[]{:S(2)}, u32[]{:S(2)}) async-start(bf16[4,144,2560]{2,1,0:T(8,128)(2,1)} %select_select_fusion.1), calls=%async_computation.2 | async-start | bytes 5898240 | tf_op jit(solution)/shard_map/all_to_all | solution.py:101
  64.9 34.2 %copy-start.4 = (bf16[2,2560,8]{1,2,0:T(8,128)(2,1)S(1)}, bf16[2,2560,8]{1,2,0:T(8,128)(2,1)}, u32[]{:S(2)}) copy-start(bf16[2,2560,8]{1,2,0:T(8,128)(2,1)} %param.10) | copy-start | bytes 245764
  91.6 103.8 %all-to-all-start = ((bf16[4,144,7680]{2,1,0:T(8,128)(2,1)}), bf16[4,144,7680]{2,1,0:T(8,128)(2,1)}, u32[]{:S(2)}, u32[]{:S(2)}) async-start(bf16[4,144,7680]{2,1,0:T(8,128)(2,1)} %select_select_fusion), calls=%async_computation | async-start | bytes 17694720 | tf_op jit(solution)/shard_map/all_to_all | solution.py:100
  97.3 244.0 %all-reduce.2.cloned.1.call-start = ((), (), s32[]{:S(2)}) async-start(), calls=%async_computation.5 | async-start | bytes 327680 | tf_op jit(solution)/shard_map/psum | solution.py:110
  246.9 1.6 copy-start.3
  247.8 95.0 %copy-start.1 = (bf16[240,2560]{1,0:T(8,128)(2,1)S(1)}, bf16[240,2560]{1,0:T(8,128)(2,1)}, u32[]{:S(2)}) copy-start(bf16[240,2560]{1,0:T(8,128)(2,1)} %param.8) | copy-start | bytes 3686404
Sparse Core Ops, SparseCore 0:
  9.6 224.9 all-gather.1
  249.4 91.8 all-reduce.1
where the time goes:
time: 350 us
  waiting for transfers between devices  239 us (68%)
  local copies, waits for them, and re-layouts  42 us (12%)
  matrix products  22.5 us (6%)
  starting transfers between devices  17 us (5%)
  other arithmetic  14.4 us (4%)
  between operations  14.3 us (4%)
    psum x1, waiting for transfers between devices, per_device(): grad_sum = lax.psum(grad_terms, ('dp', 'shard'))  92 us
    all_to_all x1, waiting for transfers between devices, per_device(): lax.all_to_all(rows_send, 'dp', split_axis=0, concat_axis=0, tiled=True)  91.3 us
    all_gather x1, waiting for transfers between devices, project(): lax.all_gather(out_weight, 'shard', axis=1, tiled=True)  28.8 us
    all_to_all x1, waiting for transfers between devices, per_device(): lax.all_to_all(resid_send, 'dp', split_axis=0, concat_axis=0, tiled=True)  26.7 us
    gather x1, local copies, waits for them, and re-layouts, per_device(): jnp.take(projected, row_index, axis=0)  22.4 us
    dot_general x1, matrix products, project(): jnp.dot(attended, lax.all_gather(out_weight, 'shard', axis=1, tiled=True)...  12.4 us
    select_n x1, other arithmetic, per_device(): jnp.where(live_rows[:, :, None], jnp.take(projected, row_index, axis=0), 0)  8.14 us
  transfers between devices with their start and end apart: 6, of which 4 were waited for; matrix products, arithmetic and copies ran while one was open for 18% of the time, Pallas kernels for 0%

commit v1 on v0

--- a/solution.py
+++ b/solution.py
@@ -7,6 +7,29 @@
 CLASSES = 8
 LMAX = 48
 TOK_DEV = 240
+
+
+def split_up(x, dim, devices):
+    before, after = (x.shape[:dim], x.shape[dim + 1 :])
+    return jnp.moveaxis(x.reshape(*before, devices, -1, *after), dim, 0)
+
+
+def laid_out(tiles, dim):
+    shape = list(tiles.shape[1:])
+    shape[dim] *= tiles.shape[0]
+    return jnp.moveaxis(tiles, 0, dim).reshape(shape)
+
+
+def rotated_exchange(array, axis, split_dim, concat_dim):
+    size, index = (lax.axis_size(axis), lax.axis_index(axis))
+    blocks = split_up(array, split_dim, size)
+    whole = blocks
+    for hop in range(1, size):
+        target, source = ((index + hop) % size, (index - hop) % size)
+        sent = lax.dynamic_index_in_dim(blocks, target, 0)
+        other = lax.ppermute(sent, axis, [(i, (i + hop) % size) for i in range(size)])
+        whole = lax.dynamic_update_slice_in_dim(whole, other, source, axis=0)
+    return laid_out(whole, concat_dim)
 
 
 def attend(blocks, block_lengths):
@@ -98,7 +121,7 @@
     )
     got_rows, got_resid = (
         lax.all_to_all(rows_send, "dp", split_axis=0, concat_axis=0, tiled=True),
-        lax.all_to_all(resid_send, "dp", split_axis=0, concat_axis=0, tiled=True),
+        rotated_exchange(resid_send, "dp", 0, 0),
     )
     lengths_recv = got_lengths.reshape(block_count)
     attended = attend(got_rows.reshape(block_count, LMAX, -1), lengths_recv)

time: 350 us -> 350 us (level)
  local copies, waits for them, and re-layouts: 42 us -> 47.9 us
    ppermute x0 -> x3, waiting for transfers between devices: none -> 110 us  [rotated_exchange(): lax.ppermute(sent, axis, [(i, (i + hop) % size) for i in range(size)])]
    all_to_all x1, waiting for transfers between devices: 91.3 us -> 0.01 us  [per_device(): lax.all_to_all(rows_send, 'dp', split_axis=0, concat_axis=0, tiled=True)]
    all_to_all x1 -> x0, waiting for transfers between devices: 26.7 us -> none  [per_device(): lax.all_to_all(resid_send, 'dp', split_axis=0, concat_axis=0, tiled=True)]
    all_gather x1, waiting for transfers between devices: 28.8 us -> 34.1 us  [project(): lax.all_gather(out_weight, 'shard', axis=1, tiled=True)]
    dynamic_update_slice x0 -> x3, local copies, waits for them, and re-layouts: none -> 4.96 us  [rotated_exchange(): whole = lax.dynamic_update_slice_in_dim(whole, other, source, axis=0)]
    all_to_all x1 -> x0, starting transfers between devices: 4.61 us -> none  [per_device(): lax.all_to_all(resid_send, 'dp', split_axis=0, concat_axis=0, tiled=True)]
  transfers between devices with their start and end apart: 6 -> 8, of which waited for: 4 -> 4; matrix products, arithmetic and copies ran while one was open for 18% -> 19% of each run, Pallas kernels for 0% -> 0%
where the time goes in v1:
time: 350 us
  waiting for transfers between devices  237 us (68%)
  local copies, waits for them, and re-layouts  47.9 us (14%)
  matrix products  20.7 us (6%)
  starting transfers between devices  15.8 us (5%)
  other arithmetic  14.5 us (4%)
  between operations  14.3 us (4%)
    ppermute x3, waiting for transfers between devices, rotated_exchange(): lax.ppermute(sent, axis, [(i, (i + hop) % size) for i in range(size)])  110 us
    psum x1, waiting for transfers between devices, per_device(): grad_sum = lax.psum(grad_terms, ('dp', 'shard'))  92.1 us
    all_gather x1, waiting for transfers between devices, project(): lax.all_gather(out_weight, 'shard', axis=1, tiled=True)  34.1 us
    gather x1, local copies, waits for them, and re-layouts, per_device(): jnp.take(projected, row_index, axis=0)  23.1 us
    dot_general x1, matrix products, project(): jnp.dot(attended, lax.all_gather(out_weight, 'shard', axis=1, tiled=True)...  12.3 us
    select_n x1, other arithmetic, per_device(): jnp.where(live_rows[:, :, None], jnp.take(projected, row_index, axis=0), 0)  8.04 us
  transfers between devices with their start and end apart: 8, of which 4 were waited for; matrix products, arithmetic and copies ran while one was open for 19% of the time, Pallas kernels for 0%

profile of v1, /device:TPU:8, one launch (start us, length us, event | category | flops | bytes accessed | tf_op | source)
XLA Modules:
  0.0 349.7 jit_solution(5329340811306819259)
XLA Ops:
  7.3 0.7 all-gather.2.cloned.1.call-update
  8.5 0.7 copy.27
  9.2 3.2 all-to-all-start.1
  13.4 3.9 %gather_fusion.2 = s32[576]{0:T(1024)S(1)} fusion(s32[240]{0:T(256)S(1)} %copy-done.2, s32[1024]{0:T(1024)S(1)} %pad_clamp_fusion), kind=kCustom, calls=%fused_computation.2 | custom fusion | bytes 6912 | tf_op jit(solution)/shard_map/jit(_take)/gather | solution.py:117
  17.5 0.6 copy.31
  18.1 23.1 %gather_fusion = bf16[576,7680]{1,0:T(8,128)(2,1)} fusion(bf16[240,7680]{1,0:T(8,128)(2,1)} %param.7, s32[1024]{0:T(1024)S(1)} %pad_clamp_fusion), kind=kCustom, calls=%fused_computation | custom fusion | bytes 17697024 | tf_op jit(solution)/shard_map/jit(_take)/gather | solution.py:115
  41.2 3.3 all-to-all-start.2
  44.5 8.0 %select_select_fusion = bf16[4,144,7680]{2,1,0:T(8,128)(2,1)} fusion(bf16[4,144,7680]{2,1,0:T(8,128)(2,1)} %bitcast.72, pred[4,144]{1,0:T(4,128)(4,1)S(1)} %get-tuple-element.11, pred[4,144]{1,0:T(4,128)(4,1)S(1)} %get-tuple-element.10), kind=kLoop, calls=%fused_computation.3 | loop fusion | flops 8847360 | bytes 17695872 | tf_op jit(solution)/shard_map/jit(_where)/select_n | solution.py:115
  52.5 5.7 %all-to-all-start = ((bf16[4,144,7680]{2,1,0:T(8,128)(2,1)}), bf16[4,144,7680]{2,1,0:T(8,128)(2,1)}, u32[]{:S(2)}, u32[]{:S(2)}) async-start(bf16[4,144,7680]{2,1,0:T(8,128)(2,1)} %select_select_fusion), calls=%async_computation | async-start | bytes 17694720 | tf_op jit(solution)/shard_map/all_to_all | solution.py:123
  58.4 4.2 %gather_fusion.1 = bf16[576,2560]{1,0:T(8,128)(2,1)} fusion(bf16[240,2560]{1,0:T(8,128)(2,1)S(1)} %copy-done, s32[1024]{0:T(1024)S(1)} %pad_clamp_fusion), kind=kCustom, calls=%fused_computation.1 | custom fusion | bytes 5900544 | tf_op jit(solution)/shard_map/jit(_take)/gather | solution.py:116
  62.6 2.3 select_select_fusion.1
  65.1 0.6 collective-permute-start
  65.6 1.7 collective-permute-start.1
  67.3 1.2 collective-permute-start.2
  68.6 2.0 select_select_fusion.2
  71.1 0.7 reduce.4
  72.1 99.6 %collective-permute-done = bf16[1,1,144,2560]{3,2,0,1:T(8,128)(2,1)} collective-permute-done((bf16[1,1,144,2560]{3,2,0,1:T(8,128)(2,1)S(1)}, bf16[1,1,144,2560]{3,2,0,1:T(8,128)(2,1)}, u32[]{:S(2)}, u32[]{:S(2)}) %collective-permute-start) | collective-permute-done | bytes 737312 | tf_op jit(solution)/shard_map/ppermute | solution.py:30
  171.8 2.0 constant_dynamic-update-slice_fusion.2
  173.8 2.0 constant_dynamic-update-slice_fusion.1
  175.8 10.0 %collective-permute-done.2 = bf16[1,1,144,2560]{3,2,0,1:T(8,128)(2,1)S(1)} collective-permute-done((bf16[1,1,144,2560]{3,2,0,1:T(8,128)(2,1)S(1)}, bf16[1,1,144,2560]{3,2,0,1:T(8,128)(2,1)S(1)}, u32[]{:S(2)}, u32[]{:S(2)}) %collective-permute-start.2) | collective-permute-done | bytes 737312 | tf_op jit(solution)/shard_map/ppermute | solution.py:30
  185.8 0.9 constant_dynamic-update-slice_fusion
  186.7 2.9 fusion.46
  190.1 4.0 %slice_bitcast_fusion.2 = (bf16[12,6,20,8,128]{4,3,2,1,0:T(8,128)(2,1)S(1)}, bf16[12,6,20,8,128]{4,3,2,1,0:T(8,128)(2,1)S(1)}, bf16[12,6,20,8,128]{4,3,2,1,0:T(8,128)(2,1)S(1)}) fusion(bf16[12,48,7680]{2,1,0:T(8,128)(2,1)} %bitcast.5), kind=kLoop, calls=%fused_computation.23 | loop fusion | bytes 17694720
  194.1 1.7 fusion
  195.9 2.0 convert_bitcast_fusion
  197.9 2.6 copy.30
  200.5 34.1 %all-gather.2.cloned.1.call-done = bf16[2560,2560]{1,0:T(8,128)(2,1)} async-done(((bf16[2560,640]{1,0:T(8,128)(2,1)}), bf16[2560,2560]{1,0:T(8,128)(2,1)}) %all-gather.2.cloned.1.call-update) | async-done | bytes 13107216 | tf_op jit(solution)/shard_map/all_gather | solution.py:66
  234.6 12.3 %multiply_convert_fusion = bf16[576,2560]{1,0:T(8,128)(2,1)S(1)} fusion(bf16[576,2560]{1,0:T(8,128)(2,1)} %bitcast.70, bf16[2560,2560]{1,0:T(8,128)(2,1)} %all-gather.2.cloned.1.call-done, bf16[72,8,20,128]{3,2,1,0:T(8,128)(2,1)} %bitcast.75, f32[576]{0:T(1024)S(1)} %reshape.370), kind=kOutput, calls=%fused_computation.4 | convolution fusion | flops 7555645440 | bytes 21956864 | tf_op jit(solution)/shard_map/dot_general | solution.py:64
  246.9 0.9 fusion.45
  248.5 0.7 pad_maximum_fusion
  249.2 92.1 %all-reduce.2.cloned.1.call-done = f32[2,2560,8]{1,2,0:T(8,128)} async-done(((f32[2,2560,8]{1,2,0:T(8,128)}), f32[2,2560,8]{1,2,0:T(8,128)}) %all-reduce.2.cloned.1.call-update) | async-done | bytes 163856 | tf_op jit(solution)/shard_map/psum | solution.py:133
  341.3 1.6 copy.65
  (59 shorter events, 4.0 us)
Async XLA Ops:
  7.2 51.2 %copy-start = (bf16[240,2560]{1,0:T(8,128)(2,1)S(1)}, bf16[240,2560]{1,0:T(8,128)(2,1)}, u32[]{:S(2)}) copy-start(bf16[240,2560]{1,0:T(8,128)(2,1)} %param.8) | copy-start | bytes 3686404
  7.2 0.8 copy-start.7
  7.2 0.9 copy-start.8
  7.2 6.2 %copy-start.2 = (s32[240]{0:T(256)S(1)}, s32[240]{0:T(256)}, u32[]{:S(2)}) copy-start(s32[240]{0:T(256)} %param.11) | copy-start | bytes 2884
  7.2 227.4 %all-gather.2.cloned.1.call-start = ((), (), s32[]{:S(2)}) async-start(), calls=%async_computation.3 | async-start | bytes 16384000 | tf_op jit(solution)/shard_map/all_gather | solution.py:66
  9.2 32.0 %all-to-all-start.1 = ((s32[4,1,3]{2,1,0:T(1,128)}), s32[4,1,3]{2,1,0:T(1,128)S(1)}, u32[]{:S(2)}, u32[]{:S(2)}) async-start(s32[4,1,3]{2,1,0:T(1,128)} %copy.27), calls=%async_computation.1 | async-start | bytes 4096 | tf_op jit(solution)/shard_map/all_to_all | solution.py:120
  41.2 11.3 %all-to-all-start.2 = ((s32[4,1,144]{2,1,0:T(1,128)}), s32[4,1,144]{2,1,0:T(1,128)S(1)}, u32[]{:S(2)}, u32[]{:S(2)}) async-start(s32[4,1,144]{2,1,0:T(1,128)} %copy.31), calls=%async_computation.2 | async-start | bytes 8192 | tf_op jit(solution)/shard_map/all_to_all | solution.py:119
  52.5 137.5 %all-to-all-start = ((bf16[4,144,7680]{2,1,0:T(8,128)(2,1)}), bf16[4,144,7680]{2,1,0:T(8,128)(2,1)}, u32[]{:S(2)}, u32[]{:S(2)}) async-start(bf16[4,144,7680]{2,1,0:T(8,128)(2,1)} %select_select_fusion), calls=%async_computation | async-start | bytes 17694720 | tf_op jit(solution)/shard_map/all_to_all | solution.py:123
  58.3 283.0 %all-reduce.2.cloned.1.call-start = ((), (), s32[]{:S(2)}) async-start(), calls=%async_computation.4 | async-start | bytes 327680 | tf_op jit(solution)/shard_map/psum | solution.py:133
  64.9 3.7 %copy-start.5 = (bf16[576,2560]{1,0:T(8,128)(2,1)S(1)}, bf16[576,2560]{1,0:T(8,128)(2,1)}, u32[]{:S(2)}) copy-start(bf16[576,2560]{1,0:T(8,128)(2,1)} %gather_fusion.1) | copy-start | bytes 8847364
  65.1 106.7 %collective-permute-start = (bf16[1,1,144,2560]{3,2,0,1:T(8,128)(2,1)S(1)}, bf16[1,1,144,2560]{3,2,0,1:T(8,128)(2,1)}, u32[]{:S(2)}, u32[]{:S(2)}) collective-permute-start(bf16[1,1,144,2560]{3,2,0,1:T(8,128)(2,1)S(1)} %get-tuple-element.9), channel_id=1, source_target_pairs={{0,4},{4,8},{8,12},{12,0},{1,5},{5,9},{9,13},{13,1},{2,6},{6,10},{... | collective-permute-start | bytes 2211848 | tf_op jit(solution)/shard_map/ppermute | solution.py:30
  65.6 108.1 %collective-permute-start.1 = (bf16[1,1,144,2560]{3,2,0,1:T(8,128)(2,1)S(1)}, bf16[1,1,144,2560]{3,2,0,1:T(8,128)(2,1)}, u32[]{:S(2)}, u32[]{:S(2)}) collective-permute-start(bf16[1,1,144,2560]{3,2,0,1:T(8,128)(2,1)S(1)} %get-tuple-element.8), channel_id=1, source_target_pairs={{0,8},{4,12},{8,0},{12,4},{1,9},{5,13},{9,1},{13,5},{2,10},{6,14},... | collective-permute-start | bytes 2211848 | tf_op jit(solution)/shard_map/ppermute | solution.py:30
  67.3 118.5 %collective-permute-start.2 = (bf16[1,1,144,2560]{3,2,0,1:T(8,128)(2,1)S(1)}, bf16[1,1,144,2560]{3,2,0,1:T(8,128)(2,1)S(1)}, u32[]{:S(2)}, u32[]{:S(2)}) collective-permute-start(bf16[1,1,144,2560]{3,2,0,1:T(8,128)(2,1)S(1)} %get-tuple-element.7), channel_id=1, source_target_pairs={{0,12},{4,0},{8,4},{12,8},{1,13},{5,1},{9,5},{13,9},{2,14},{6,2},{... | collective-permute-start | bytes 2211848 | tf_op jit(solution)/shard_map/ppermute | solution.py:30
  70.6 116.1 %copy-start.6 = (bf16[2,2560,8]{1,2,0:T(8,128)(2,1)S(1)}, bf16[2,2560,8]{1,2,0:T(8,128)(2,1)}, u32[]{:S(2)}) copy-start(bf16[2,2560,8]{1,2,0:T(8,128)(2,1)} %param.10) | copy-start | bytes 245764
  186.7 2.9 copy-start.3
  246.9 1.6 copy-start.4
  247.8 95.1 %copy-start.1 = (bf16[240,2560]{1,0:T(8,128)(2,1)S(1)}, bf16[240,2560]{1,0:T(8,128)(2,1)}, u32[]{:S(2)}) copy-start(bf16[240,2560]{1,0:T(8,128)(2,1)} %param.8) | copy-start | bytes 3686404
Sparse Core Ops, SparseCore 0:
  9.6 224.9 all-gather.1
  249.3 91.9 all-reduce.1
